TPU v7x, 512 devices: a whole 4x4x16 slice. The times are simulated.
512 devices in a mesh: var: 128 (over y, x, z_lo, core), samp: 4 (over z_hi).
Axes of the slice: x: 4, y: 4, z: 16 (z_hi: 4, z_lo: 4; z = z_hi * 4 + z_lo), core: 2. Of those that a mesh axis runs over, the one named last changes fastest.
Arguments:
- dosages: int32 [1024, 131072], P('samp', 'var'), may hold values from 0 to 3, as said below
- weights: bfloat16 [131072, 2560], P(('var', 'samp')), may hold values from -0.0625 to 0.0625
- variant_pass: int32 [131072], P('var'), may hold values 0 or 1
- ancestry: float32 [1024, 20], P('samp')
Outputs:
- standardized: float32 [2560, 1024], P('var', 'samp')
Inputs may be any that keep to these rules, and one draw needn't show every extreme that they name: 3 marks a missing call; other values are allele dosages.
All inputs are finite; a program needn't handle non-finite values. No bound on the sum of `variant_pass` on one device may be relied on, other than what follows from the above.
Results may differ from a plain program's by a relative error of at most 0.0024.
Values may be sent and summed in bfloat16 or wider, within the bound.
A program may use at most 64 MiB of HBM per device.

v0:
```python
import jax
import jax.numpy as jnp
from jax import lax
from jax.sharding import PartitionSpec as P


def cholesky_apply(gram, cross):
    factor = jnp.linalg.cholesky(gram)
    order_n = gram.shape[0]
    forward = []
    for row_idx in range(order_n):
        running = cross[:, row_idx]
        for col_idx in range(row_idx):
            running = running - factor[row_idx, col_idx] * forward[col_idx]
        forward.append(running / factor[row_idx, row_idx])
    solved = [None] * order_n
    for row_idx in reversed(range(order_n)):
        running = forward[row_idx]
        for col_idx in range(row_idx + 1, order_n):
            running = running - factor[col_idx, row_idx] * solved[col_idx]
        solved[row_idx] = running / factor[row_idx, row_idx]
    return jnp.stack(solved, axis=1)


def on_device(dosages, weights, variant_pass, ancestry):
    samples_here = dosages.shape[0]
    total_samples = samples_here * lax.axis_size("samp")
    observed = dosages < 3
    allele_total, observed_count = lax.psum(
        (
            jnp.sum(jnp.where(observed, dosages, 0).astype(jnp.float32), axis=0),
            jnp.sum(observed.astype(jnp.float32), axis=0),
        ),
        "samp",
    )
    impute = ((allele_total + 1.0) / (observed_count + 1.0)).astype(jnp.bfloat16)
    genotypes = jnp.where(observed, dosages.astype(jnp.bfloat16), impute[None, :])
    genotypes = genotypes * variant_pass.astype(jnp.bfloat16)[None, :]
    full_weights = lax.all_gather(weights, "samp", axis=0, tiled=True)
    every_score = lax.dot_general(
        full_weights, genotypes, (((0,), (1,)), ((), ())), preferred_element_type=jnp.float32
    )
    raw_scores = lax.psum_scatter(every_score, "var", scatter_dimension=0, tiled=True)
    design = jnp.concatenate([jnp.ones((samples_here, 1), jnp.float32), ancestry], axis=1)
    local_gram = jnp.dot(design.T, design, precision=lax.Precision.HIGHEST)
    local_cross = jnp.dot(raw_scores, design, precision=lax.Precision.HIGHEST)
    gram = lax.psum(local_gram, "samp")
    cross = lax.psum(local_cross, "samp")
    coeffs = cholesky_apply(gram, cross)
    residual = raw_scores - jnp.dot(coeffs, design.T, precision=lax.Precision.HIGHEST)
    squared = lax.psum(jnp.sum(residual * residual, axis=1), "samp")
    spread = squared / (total_samples - 1)
    return residual / jnp.sqrt(spread + 1e-06)[:, None]


def solution(mesh):
    in_specs = (P("samp", "var"), P(("var", "samp"), None), P("var"), P("samp", None))
    out_specs = P("var", "samp")
    return jax.shard_map(
        on_device, mesh=mesh, in_specs=in_specs, out_specs=out_specs, check_vma=False
    )
```

profile of v0, /device:TPU:1, one launch (start us, length us, event | category | flops | bytes accessed | tf_op | source)
XLA Modules:
  0.0 2035.1 jit_solution(5791186550489858896)
XLA Ops:
  6.5 0.0 all-gather.2.cloned.1.call-start
  6.5 0.7 all-gather.2.cloned.1.call-update
  7.3 0.0 all-reduce.6.cloned.1.call-start
  7.3 0.7 convert_element_type.19
  8.0 1.4 convert_reduce_fusion.1
  9.4 20.2 all-reduce.3
  29.6 182.8 %all-gather.2.cloned.1.call-done = bf16[1024,2560]{1,0:T(8,128)(2,1)} async-done(((bf16[256,2560]{1,0:T(8,128)(2,1)}), bf16[1024,2560]{1,0:T(8,128)(2,1)}) %all-gather.2.cloned.1.call-update) | async-done | bytes 5242896 | tf_op jit(solution)/shard_map/all_gather | solution.py:39
  212.5 6.2 convolution_bitcast_fusion
  218.6 0.0 copy-start
  218.6 0.0 all-reduce.6.cloned.1.call-update
  218.7 1.3 dynamic-slice
  220.6 0.0 copy-done
  220.6 0.1 fusion.6
  220.8 1285.7 %all-reduce.6.cloned.1.call-done = f32[2560,256]{0,1:T(8,128)} async-done(((f32[2560,256]{0,1:T(8,128)}), f32[2560,256]{0,1:T(8,128)}) %all-reduce.6.cloned.1.call-update) | async-done | bytes 2621456
  1506.5 1.0 constant_dynamic-slice_fusion
  1507.5 0.2 fusion.8
  1507.7 21.3 %all-reduce.2 = (f32[20,21]{0,1:T(8,128)S(1)}, f32[21,21]{0,1:T(8,128)S(1)}) all-reduce(f32[20,21]{0,1:T(8,128)S(1)} %fusion.8, f32[21,21]{0,1:T(8,128)S(1)} %fusion.6), channel_id=1, replica_groups=mesh['var'=128,'samp'=4] {'samp'}, use_global_device_ids=true, to_apply=%region_5.6 | all-reduce | flops 861 | bytes 6888 | tf_op jit(solution)/shard_map/psum | solution.py:48
  1529.1 0.1 copy.42
  1529.2 1.9 cholesky.18
  1531.1 0.6 compare_reduce_fusion
  1531.8 0.6 select_select_fusion
  1532.4 0.7 fusion.84
  1533.1 0.7 fusion.83
  1533.9 0.7 fusion.82
  1534.6 0.7 fusion.90
  1535.3 0.7 fusion.91
  1536.0 0.7 fusion.89
  1536.8 0.7 fusion.81
  1537.5 0.7 fusion.86
  1538.2 0.7 fusion.85
  1539.0 0.7 fusion.87
  1539.7 0.7 fusion.88
  1540.4 0.7 fusion.92
  1541.1 0.7 fusion.80
  1541.8 0.1 copy.43
  1543.1 131.0 %subtract_divide_fusion.13 = (f32[20,1]{0,1:T(1,128)S(1)}, f32[20,1]{0,1:T(1,128)S(1)}, f32[20,1]{0,1:T(1,128)S(1)}, f32[20,1]{0,1:T(1,128)S(1)}, f32[20,1]{0,1:...) fusion(f32[20,21]{0,1:T(8,128)S(1)} %get-tuple-element.7, ...), kind=kLoop, calls=%fused_computation.141 | loop fusion | flops 8000 | bytes 4040 | tf_op jit(solution)/shard_map/div | solution.py:15
  1674.1 130.2 %subtract_divide_fusion.52 = (f32[20]{0:T(128)S(1)}, f32[20]{0:T(128)S(1)}, f32[20]{0:T(128)S(1)}, f32[20]{0:T(128)S(1)}, f32[20]{0:T(128)S(1)}, /*index=5*/f32[...) fusion(f32[20,1]{0,1:T(1,128)S(1)} %get-tuple-element.43, ...), kind=kLoop, calls=%fused_computation.181 | loop fusion | flops 7980 | bytes 3956 | tf_op jit(solution)/shard_map/div | solution.py:15
  1804.3 61.1 %subtract_divide_fusion.39 = (f32[20]{0:T(128)S(1)}, f32[20]{0:T(128)S(1)}, f32[20]{0:T(128)S(1)}, f32[20]{0:T(128)S(1)}, f32[20]{0:T(128)S(1)}, /*index=5*/f32[...) fusion(f32[20]{0:T(128)S(1)} %get-tuple-element.76, ...), kind=kLoop, calls=%fused_computation.168 | loop fusion | flops 4180 | bytes 3116 | tf_op jit(solution)/shard_map/div | solution.py:21
  1865.4 87.1 %divide_bitcast_fusion = (f32[20,1]{0,1:T(1,128)S(1)}, f32[20]{0:T(128)S(1)}, f32[20]{0:T(128)S(1)}, f32[20]{0:T(128)S(1)}, f32[20]{0:T(128)S(1)}, /*index=5*/f32[20]{0:T(128)S(1)}, f32[20]{0:T(128)S(1)}, f32[20]{0:T(128)S(1)}) fusion(f32[20]{0:T(128)S(1)} %get-tuple-element.64, f32[20]{0:T(128)S(1)} %get-tuple-element.63, f32[20]{0:T(128)S(1)} %get-tuple-element.62, ...), kind=kLoop, calls=%fused_computation.160 | loop fusion | flops 5440 | bytes 2880 | tf_op jit(solution)/shard_map/stack | solution.py:22
  1952.6 61.1 %subtract_divide_fusion = (f32[20,1]{0,1:T(1,128)S(1)}, f32[20,1]{0,1:T(1,128)S(1)}, f32[20,1]{0,1:T(1,128)S(1)}, f32[20,1]{0,1:T(1,128)S(1)}, f32[20,1]{0,1:T(1...) fusion(f32[20,1]{0,1:T(1,128)S(1)} %get-tuple-element.35, ...), kind=kLoop, calls=%fused_computation.128 | loop fusion | flops 4180 | bytes 3116 | tf_op jit(solution)/shard_map/div | solution.py:21
  2013.7 0.1 stack.48
  2013.8 0.3 multiply_reduce_fusion
  2014.1 13.5 psum.39
  2027.6 0.7 broadcast_divide_fusion
  (4 shorter events, 0.1 us)
Async XLA Ops:
  6.5 205.9 %all-gather.2.cloned.1.call-start = ((), (), s32[]{:S(2)}) async-start(), calls=%async_computation | async-start | bytes 6553600 | tf_op jit(solution)/shard_map/all_gather | solution.py:39
  7.3 1499.2 %all-reduce.6.cloned.1.call-start = ((), (), s32[]{:S(2)}) async-start(), calls=%async_computation.1 | async-start | bytes 5242880
  218.6 2.0 copy-start
Sparse Core Ops, SparseCore 0:
  9.5 202.9 all-gather.1
  218.8 1287.6 all-reduce.5
where the time goes:
time: 2040 us
  waiting for transfers between devices  1470 us (72%)
  other arithmetic  477 us (23%)
  blocking collectives  55 us (3%)
    unnamed x3, waiting for transfers between devices  1290 us
    div x2, other arithmetic, cholesky_apply(): forward.append(running / factor[row_idx, row_idx])  261 us
    all_gather x1, waiting for transfers between devices, on_device(): full_weights = lax.all_gather(weights, 'samp', axis=0, tiled=True)  183 us
    div x2, other arithmetic, cholesky_apply(): solved[row_idx] = running / factor[row_idx, row_idx]  122 us
    another operation x1, other arithmetic, cholesky_apply(): return jnp.stack(solved, axis=1)  87.1 us
  transfers between devices with their start and end apart: 2, of which 2 were waited for; matrix products, arithmetic and copies ran while one was open for 0% of the time, Pallas kernels for 0%

commit v1 on v0

v1 whole, which is shorter than its diff:
```python
import jax
import jax.numpy as jnp
from jax import lax
from jax.experimental import pallas as pl
from jax.experimental.pallas import tpu as pltpu
from jax.sharding import PartitionSpec as P

F32 = jnp.float32
BF16 = jnp.bfloat16
HI = lax.Precision.HIGHEST
OFFSETS = (0, 1, 3, 2)
LANES_TO_LANES = (((1,), (1,)), ((), ()))


def inverse_factor(gram):
    rows = lax.broadcasted_iota(jnp.int32, gram.shape, 0)
    lanes = lax.broadcasted_iota(jnp.int32, gram.shape, 1)
    work = jnp.where(lanes < 21, gram, 0.0) + jnp.where(lanes == rows + 64, 1.0, 0.0)
    for k in range(21):
        scale = 1.0 / jnp.sqrt(work[k : k + 1, k : k + 1])
        row = work[k : k + 1, :] * scale
        column = work[:, k : k + 1] * scale
        work = jnp.where(rows > k, work - column * row, jnp.where(rows == k, row, work))
    return jnp.where(lanes >= 64, work, 0.0)


def kernel(
    dos_ref, w_ref, pass_ref, anc_ref, out_ref,
    wt, ds, dr, ts, tr, vec, geno, s, r, zs, zr, design, gl, gr, qt, st, sr,
    w_sem, d_send, d_recv, t_send, t_recv, g_send, g_recv, xy_send, xy_recv, z_send, z_recv,
    st_send, st_recv,
):
    v, zh = lax.axis_index("var"), lax.axis_index("samp")
    core, zl = lax.rem(v, 2), lax.rem(v // 2, 4)
    x, y = lax.rem(v // 8, 4), v // 32
    z = zh * 4 + zl
    plane = y * 4 + x

    def at(plane_to, z_to, core_to):
        return {"var": (plane_to * 4 + lax.rem(z_to, 4)) * 2 + core_to, "samp": z_to // 4}

    def remote(src, dst, send, recv, to):
        return pltpu.make_async_remote_copy(
            src_ref=src, dst_ref=dst, send_sem=send, recv_sem=recv,
            device_id=to, device_id_type=pl.DeviceIdType.MESH,
        )

    barrier = pltpu.get_barrier_semaphore()

    @pl.loop(1, 16)
    def _(step):
        pl.semaphore_signal(
            barrier, inc=1, device_id=at(lax.rem(plane + step, 16), z, core),
            device_id_type=pl.DeviceIdType.MESH,
        )

    @pl.loop(1, 32)
    def _(step):
        other = lax.rem(z * 2 + core + step, 32)
        pl.semaphore_signal(
            barrier, inc=1, device_id=at(plane, other // 2, lax.rem(other, 2)),
            device_id_type=pl.DeviceIdType.MESH,
        )

    for part in range(4):
        tile = []
        for half in range(2):
            piece = dos_ref[:, pl.ds(part * 256 + half * 128, 128)]
            seen = piece < 3
            tile.append(
                (
                    jnp.sum(jnp.where(seen, piece, 0), axis=0, keepdims=True).astype(F32),
                    jnp.sum(seen.astype(jnp.int32), axis=0, keepdims=True).astype(F32),
                )
            )
            narrow = piece.astype(F32).astype(BF16)
            for upper in range(2):
                ds[part, upper, :, pl.ds(half * 128, 128)] = narrow[upper * 128 : upper * 128 + 128]
        for half in range(2):
            ts[part, half : half + 1, :] = tile[half][0]
            ts[part, 2 + half : 3 + half, :] = tile[half][1]
            ts[part, 4 + half : 5 + half, :] = pass_ref[
                2 * part + half : 2 * part + half + 1, :
            ].astype(F32)
            ts[part, 6 + half : 7 + half, :] = jnp.zeros((1, 128), F32)
    for column in range(10):
        wt[0, pl.ds(column * 256, 256), :] = w_ref[:, pl.ds(column * 256, 256)].T
    lanes = lax.broadcasted_iota(jnp.int32, (256, 128), 1)
    design[...] = jnp.where((lanes == 20) | (lanes == 84), 1.0, 0.0)
    design[:, 0:20] = anc_ref[...]
    design[:, 64:84] = anc_ref[...]
    gl[...] = lax.dot_general(
        design[...], design[...], (((0,), (0,)), ((), ())), precision=HI,
        preferred_element_type=F32,
    )[0:24]
    dr[0, 0] = ds[zh, core]
    tr[0, 0] = ts[zh]

    pl.semaphore_wait(barrier, 46)

    def totals_copy(b, k):
        to_zh, to_core = lax.rem(zh + 4 - OFFSETS[b], 4), lax.rem(core + k, 2)
        return remote(
            ts.at[to_zh], tr.at[b, k], t_send.at[b, k], t_recv.at[b, k],
            at(plane, to_zh * 4 + zl, to_core),
        )

    def dosage_copy(b, k):
        to_zh, to_core = lax.rem(zh + 4 - OFFSETS[b], 4), lax.rem(core + k, 2)
        return remote(
            ds.at[to_zh, to_core], dr.at[b, k], d_send.at[b, k], d_recv.at[b, k],
            at(plane, to_zh * 4 + zl, to_core),
        )

    def small_copy(b, src, dst, send, recv):
        to_zh = lax.rem(zh + 4 - OFFSETS[b], 4)
        return remote(src, dst.at[b], send.at[b], recv.at[b], at(plane, to_zh * 4 + zl, core))

    def gram_copy(b):
        return small_copy(b, gl, gr, g_send, g_recv)

    def stat_copy(b):
        return small_copy(b, st, sr, st_send, st_recv)

    pieces = [(b, k) for b in (3, 1, 2, 0) for k in range(2) if b or k]
    weight_copy = remote(wt.at[0], wt.at[1], w_sem.at[0], w_sem.at[1], at(plane, z, 1 - core))
    for b, k in pieces:
        totals_copy(b, k).start()
    dosage_copy(0, 1).start()
    weight_copy.start()
    for b in (1, 2, 3):
        for k in range(2):
            dosage_copy(b, k).start()
    for b in (1, 2, 3):
        gram_copy(b).start()

    for b, k in pieces:
        totals_copy(b, k).wait_recv()
    for k in range(2):
        total = tr[0, k] + tr[1, k] + tr[2, k] + tr[3, k]
        for half in range(2):
            impute = (total[half : half + 1] + 1.0) / (total[2 + half : 3 + half] + 1.0)
            impute = impute.astype(BF16).astype(F32)
            centre = jnp.floor(impute * 4.0 + 0.5) * 0.25
            passed = tr[0, k, 4 + half : 5 + half, :]
            vec[k, half, 0:1, :] = centre
            vec[k, half, 1:2, :] = (impute - centre) * passed
            vec[k, half, 2:3, :] = passed

    def xy_copy(b, dy, dx):
        to = lax.rem(y + dy, 4) * 4 + lax.rem(x + dx, 4)
        return remote(
            s.at[b, pl.ds(to * 160, 160)], r.at[b, dy * 4 + dx],
            xy_send.at[b, dy * 4 + dx], xy_recv.at[b, dy * 4 + dx], at(to, z, core),
        )

    def multiply(b):
        for k in range(2):
            if b or k:
                dosage_copy(b, k).wait_recv()
            for half in range(2):
                dose = dr[b, k, :, pl.ds(half * 128, 128)].astype(F32)
                centre, missing = vec[k, half, 0:1, :], vec[k, half, 1:2, :]
                passed = vec[k, half, 2:3, :]
                geno[k, :, pl.ds(half * 128, 128)] = jnp.where(
                    dose < 2.5, (dose - centre) * passed, missing
                ).astype(BF16)
        if b == 0:
            weight_copy.wait_recv()

        @pl.loop(0, 4)
        def _(dy):
            rows = pl.ds(pl.multiple_of(lax.rem(y + dy, 4) * 640, 640), 640)
            s[b, rows, :] = (
                lax.dot_general(wt[0, rows, :], geno[0], LANES_TO_LANES, preferred_element_type=F32)
                + lax.dot_general(wt[1, rows, :], geno[1], LANES_TO_LANES, preferred_element_type=F32)
            ).astype(BF16)
            for dx in (1, 2, 3):
                xy_copy(b, dy, dx).start()

            @pl.when(dy > 0)
            def _():
                xy_copy(b, dy, 0).start()

    def z_copy(b, group):
        to_zh = lax.rem(zh + OFFSETS[b], 4)
        return remote(
            zs.at[b, group], zr.at[core, z], z_send.at[b, group], z_recv.at[core, z],
            at(plane, to_zh * 4 + group // 2, lax.rem(group, 2)),
        )

    mine = zl * 2 + core

    def reduce_plane(b):
        @pl.loop(1, 16)
        def _(step):
            xy_copy(b, step // 4, lax.rem(step, 4)).wait_recv()

        total = s[b, pl.ds(pl.multiple_of(plane * 160, 160), 160), :].astype(F32)
        for step in range(1, 16):
            total += r[b, step].astype(F32)
        for group in range(8):
            zs[b, group] = jnp.concatenate(
                [total[group * 20 : group * 20 + 20], jnp.zeros((4, 128), F32)], axis=0
            )
        if b == 0:
            zr[core, z] = zs[0, mine]

            @pl.loop(1, 8)
            def _(step):
                z_copy(0, lax.rem(mine + step, 8)).start()
        else:

            @pl.loop(0, 8)
            def _(step):
                z_copy(b, lax.rem(mine + step, 8)).start()

    multiply(0)
    for b in (1, 2, 3):
        gram_copy(b).wait_recv()
    inverse = inverse_factor(gl[...] + gr[1] + gr[2] + gr[3])
    qt[...] = jnp.zeros_like(qt)
    qt[0:24, :] = lax.dot_general(
        inverse, design[...], LANES_TO_LANES, precision=HI, preferred_element_type=F32
    )
    multiply(1)
    reduce_plane(0)
    multiply(2)
    reduce_plane(1)
    multiply(3)
    reduce_plane(2)
    reduce_plane(3)

    @pl.loop(1, 32)
    def _(step):
        other = lax.rem(z * 2 + core + step, 32)
        z_from, core_from = other // 2, lax.rem(other, 2)
        remote(
            zs.at[0, 0], zr.at[core_from, z_from], z_send.at[0, 0],
            z_recv.at[core_from, z_from], at(plane, z, 1 - core),
        ).wait_recv()

    raw = []
    for half in range(2):
        total = zr[half, 0]
        for source in range(1, 16):
            total += zr[half, source]
        raw.append(total)
    lane = lax.broadcasted_iota(jnp.int32, (24, 128), 1)
    cross = jnp.zeros((24, 128), F32)
    squares = jnp.zeros((24, 1), F32)
    for half in range(2):
        cross += lax.dot_general(
            raw[half], qt[:, pl.ds(half * 128, 128)], LANES_TO_LANES, precision=HI,
            preferred_element_type=F32,
        )
        squares += jnp.sum(raw[half] * raw[half], axis=1, keepdims=True)
    st[...] = jnp.where(lane == 32, squares, cross)
    for b in (3, 1, 2):
        stat_copy(b).start()
    for b in (1, 2, 3):
        stat_copy(b).wait_recv()
    stats = st[...] + sr[1] + sr[2] + sr[3]
    cross = jnp.where(lane < 24, stats, 0.0)
    squares = jnp.sum(jnp.where(lane == 32, stats, 0.0) - cross * cross, axis=1, keepdims=True)
    spread = jnp.maximum(squares, 0.0) / 1023.0
    scale = 1.0 / jnp.sqrt(spread + 1e-06)
    for half in range(2):
        fitted = jnp.dot(
            cross, qt[:, pl.ds(half * 128, 128)], precision=HI, preferred_element_type=F32
        )
        out_ref[:, pl.ds(half * 128, 128)] = ((raw[half] - fitted) * scale)[0:20]

    weight_copy.wait_send()
    for b, k in pieces:
        totals_copy(b, k).wait_send()
        dosage_copy(b, k).wait_send()
    for b in (1, 2, 3):
        gram_copy(b).wait_send()
        stat_copy(b).wait_send()
    for b in range(4):

        @pl.loop(1, 16)
        def _(step):
            xy_copy(b, step // 4, lax.rem(step, 4)).wait_send()

        @pl.loop(0 if b else 1, 8)
        def _(step):
            z_copy(b, lax.rem(mine + step, 8)).wait_send()


def on_device(dosages, weights, variant_pass, ancestry):
    dma = pltpu.SemaphoreType.DMA
    vmem = pl.BlockSpec(memory_space=pltpu.VMEM)
    return pl.pallas_call(
        kernel,
        out_shape=jax.ShapeDtypeStruct((20, 256), F32),
        in_specs=[vmem] * 4,
        out_specs=vmem,
        scratch_shapes=[
            pltpu.VMEM((2, 2560, 256), BF16),
            pltpu.VMEM((4, 2, 128, 256), BF16),
            pltpu.VMEM((4, 2, 128, 256), BF16),
            pltpu.VMEM((4, 8, 128), F32),
            pltpu.VMEM((4, 2, 8, 128), F32),
            pltpu.VMEM((2, 2, 8, 128), F32),
            pltpu.VMEM((2, 128, 256), BF16),
            pltpu.VMEM((4, 2560, 128), BF16),
            pltpu.VMEM((4, 16, 160, 128), BF16),
            pltpu.VMEM((4, 8, 24, 128), F32),
            pltpu.VMEM((2, 16, 24, 128), F32),
            pltpu.VMEM((256, 128), F32),
            pltpu.VMEM((24, 128), F32),
            pltpu.VMEM((4, 24, 128), F32),
            pltpu.VMEM((128, 256), F32),
            pltpu.VMEM((24, 128), F32),
            pltpu.VMEM((4, 24, 128), F32),
            dma((2,)),
            dma((4, 2)), dma((4, 2)), dma((4, 2)), dma((4, 2)),
            dma((4,)), dma((4,)),
            dma((4, 16)), dma((4, 16)),
            dma((4, 8)), dma((2, 16)),
            dma((4,)), dma((4,)),
        ],
        compiler_params=pltpu.CompilerParams(
            collective_id=0, has_side_effects=True, vmem_limit_bytes=40 << 20
        ),
        name="polygenic",
    )(dosages, weights, variant_pass.reshape(8, 128), ancestry)


def solution(mesh):
    in_specs = (P("samp", "var"), P(("var", "samp"), None), P("var"), P("samp", None))
    return jax.shard_map(
        on_device, mesh=mesh, in_specs=in_specs, out_specs=P("var", "samp"), check_vma=False
    )
```

time: 2040 us -> 100 us (0.05)
  the two profiles are of different devices: /device:TPU:1 before, /device:TPU:38 now
where the time goes in v1:
time: 100 us
  Pallas kernels  95.4 us (95%)
  local copies, waits for them, and re-layouts  4.68 us (5%)
    pallas_call x1, Pallas kernels, on_device(): pl.pallas_call(kernel, out_shape=jax.ShapeDtypeStruct((20, 256), F32), in...  95.4 us
    unnamed x8, local copies, waits for them, and re-layouts  4.68 us

profile of v1, /device:TPU:38, one launch (start us, length us, event | category | flops | bytes accessed | tf_op | source)
XLA Modules:
  0.0 100.1 jit_solution(3552714891160206426)
XLA Ops:
  0.0 0.8 copy.5.anc_ref
  0.8 0.0 copy-start
  0.9 1.3 %copy-done = bf16[256,2560]{1,0:T(8,128)(2,1)S(1)} copy-done((bf16[256,2560]{1,0:T(8,128)(2,1)S(1)}, bf16[256,2560]{1,0:T(8,128)(2,1)}, u32[]{:S(2)}) %copy-start) | copy-done | bytes 1310744
  2.2 0.0 copy-start.1
  2.2 1.2 %copy-done.1 = s32[256,1024]{1,0:T(8,128)S(1)} copy-done((s32[256,1024]{1,0:T(8,128)S(1)}, s32[256,1024]{1,0:T(8,128)}, u32[]{:S(2)}) %copy-start.1) | copy-done | bytes 1048600
  3.4 0.0 copy-start.2
  3.4 0.7 copy-done.2
  4.1 95.4 %polygenic.1 = f32[20,256]{1,0:T(8,128)S(1)} custom-call(s32[256,1024]{1,0:T(8,128)S(1)} %copy-done.1, bf16[256,2560]{1,0:T(8,128)(2,1)S(1)} %copy-done, s32[8,128]{1,0:T(8,128)S(1)} %bitcast.1, f32[256,20]{1,0:T(8,128)S(1)} %copy.5.anc_ref), custom_call_target="tpu_custom_call" | custom-call | tf_op jit(solution)/shard_map/polygenic/pallas_call | solution.py:295
  99.5 0.6 copy.7
Async XLA Ops:
  0.8 1.3 %copy-start = (bf16[256,2560]{1,0:T(8,128)(2,1)S(1)}, bf16[256,2560]{1,0:T(8,128)(2,1)}, u32[]{:S(2)}) copy-start(bf16[256,2560]{1,0:T(8,128)(2,1)} %w_ref.1) | copy-start | bytes 3932164
  2.2 1.2 %copy-start.1 = (s32[256,1024]{1,0:T(8,128)S(1)}, s32[256,1024]{1,0:T(8,128)}, u32[]{:S(2)}) copy-start(s32[256,1024]{1,0:T(8,128)} %dos_ref.1) | copy-start | bytes 3145732
  3.4 0.7 copy-start.2

commit v2 on v1

--- a/solution.py
+++ b/solution.py
@@ -10,6 +10,15 @@
 HI = lax.Precision.HIGHEST
 OFFSETS = (0, 1, 3, 2)
 LANES_TO_LANES = (((1,), (1,)), ((), ()))
+
+
+def pack(wide):
+    return wide[0:8] + pltpu.roll(wide[8:16], 32, 1) + pltpu.roll(wide[16:24], 64, 1)
+
+
+def unpack(tile):
+    rows = jnp.concatenate([tile, pltpu.roll(tile, 96, 1), pltpu.roll(tile, 64, 1)], axis=0)
+    return jnp.where(lax.broadcasted_iota(jnp.int32, (24, 128), 1) < 32, rows, 0.0)
 
 
 def inverse_factor(gram):
@@ -25,9 +34,10 @@
 
 
 def kernel(
-    dos_ref, w_ref, pass_ref, anc_ref, out_ref,
+    dos_hbm, w_hbm, pass_hbm, anc_hbm, out_ref,
+    dos_ref, w_ref, pass_ref, anc_ref,
     wt, ds, dr, ts, tr, vec, geno, s, r, zs, zr, design, gl, gr, qt, st, sr,
-    w_sem, d_send, d_recv, t_send, t_recv, g_send, g_recv, xy_send, xy_recv, z_send, z_recv,
+    in_sem, w_sem, d_send, d_recv, t_send, t_recv, g_send, g_recv, xy_send, xy_recv, z_send, z_recv,
     st_send, st_recv,
 ):
     v, zh = lax.axis_index("var"), lax.axis_index("samp")
@@ -45,6 +55,14 @@
             device_id=to, device_id_type=pl.DeviceIdType.MESH,
         )
 
+    loads = [
+        pltpu.make_async_copy(src, dst, in_sem.at[i])
+        for i, (src, dst) in enumerate(
+            ((dos_hbm, dos_ref), (pass_hbm, pass_ref), (anc_hbm, anc_ref), (w_hbm, w_ref))
+        )
+    ]
+    for load in loads:
+        load.start()
     barrier = pltpu.get_barrier_semaphore()
 
     @pl.loop(1, 16)
@@ -62,6 +80,8 @@
             device_id_type=pl.DeviceIdType.MESH,
         )
 
+    loads[0].wait()
+    loads[1].wait()
     for part in range(4):
         tile = []
         for half in range(2):
@@ -83,16 +103,19 @@
                 2 * part + half : 2 * part + half + 1, :
             ].astype(F32)
             ts[part, 6 + half : 7 + half, :] = jnp.zeros((1, 128), F32)
+    loads[2].wait()
+    design[...] = jnp.zeros_like(design)
+    for row in (0, 64):
+        design[row : row + 20, :] = anc_ref[...]
+        design[row + 20 : row + 21, :] = jnp.ones((1, 256), F32)
+    lane = lax.broadcasted_iota(jnp.int32, (24, 128), 1)
+    gram = lax.dot_general(
+        design[0:24, :], design[...], LANES_TO_LANES, precision=HI, preferred_element_type=F32
+    )
+    gl[...] = pack(jnp.where(lane < 32, gram, 0.0))
+    loads[3].wait()
     for column in range(10):
         wt[0, pl.ds(column * 256, 256), :] = w_ref[:, pl.ds(column * 256, 256)].T
-    lanes = lax.broadcasted_iota(jnp.int32, (256, 128), 1)
-    design[...] = jnp.where((lanes == 20) | (lanes == 84), 1.0, 0.0)
-    design[:, 0:20] = anc_ref[...]
-    design[:, 64:84] = anc_ref[...]
-    gl[...] = lax.dot_general(
-        design[...], design[...], (((0,), (0,)), ((), ())), precision=HI,
-        preferred_element_type=F32,
-    )[0:24]
     dr[0, 0] = ds[zh, core]
     tr[0, 0] = ts[zh]
 
@@ -128,8 +151,8 @@
         totals_copy(b, k).start()
     dosage_copy(0, 1).start()
     weight_copy.start()
-    for b in (1, 2, 3):
-        for k in range(2):
+    for k in range(2):
+        for b in (1, 2):
             dosage_copy(b, k).start()
     for b in (1, 2, 3):
         gram_copy(b).start()
@@ -206,30 +229,33 @@
         if b == 0:
             zr[core, z] = zs[0, mine]
 
-            @pl.loop(1, 8)
-            def _(step):
-                z_copy(0, lax.rem(mine + step, 8)).start()
-        else:
-
-            @pl.loop(0, 8)
-            def _(step):
-                z_copy(b, lax.rem(mine + step, 8)).start()
+    def send_along(b):
+        @pl.loop(0 if b else 1, 8)
+        def _(step):
+            z_copy(b, lax.rem(mine + step, 8)).start()
 
     multiply(0)
+    for b in (1, 2):
+        for k in range(2):
+            dosage_copy(b, k).wait_send()
+    for k in range(2):
+        dosage_copy(3, k).start()
     for b in (1, 2, 3):
         gram_copy(b).wait_recv()
-    inverse = inverse_factor(gl[...] + gr[1] + gr[2] + gr[3])
+    inverse = inverse_factor(unpack(gl[...] + gr[1] + gr[2] + gr[3]))
     qt[...] = jnp.zeros_like(qt)
-    qt[0:24, :] = lax.dot_general(
-        inverse, design[...], LANES_TO_LANES, precision=HI, preferred_element_type=F32
-    )
+    qt[0:24, :] = jnp.dot(inverse, design[...], precision=HI, preferred_element_type=F32)
     multiply(1)
+    multiply(2)
     reduce_plane(0)
-    multiply(2)
     reduce_plane(1)
     multiply(3)
+    send_along(0)
+    send_along(1)
     reduce_plane(2)
+    send_along(2)
     reduce_plane(3)
+    send_along(3)
 
     @pl.loop(1, 32)
     def _(step):
@@ -246,7 +272,6 @@
         for source in range(1, 16):
             total += zr[half, source]
         raw.append(total)
-    lane = lax.broadcasted_iota(jnp.int32, (24, 128), 1)
     cross = jnp.zeros((24, 128), F32)
     squares = jnp.zeros((24, 1), F32)
     for half in range(2):
@@ -255,14 +280,14 @@
             preferred_element_type=F32,
         )
         squares += jnp.sum(raw[half] * raw[half], axis=1, keepdims=True)
-    st[...] = jnp.where(lane == 32, squares, cross)
+    st[...] = pack(jnp.where(lane == 24, squares, cross))
     for b in (3, 1, 2):
         stat_copy(b).start()
     for b in (1, 2, 3):
         stat_copy(b).wait_recv()
-    stats = st[...] + sr[1] + sr[2] + sr[3]
+    stats = unpack(st[...] + sr[1] + sr[2] + sr[3])
     cross = jnp.where(lane < 24, stats, 0.0)
-    squares = jnp.sum(jnp.where(lane == 32, stats, 0.0) - cross * cross, axis=1, keepdims=True)
+    squares = jnp.sum(jnp.where(lane == 24, stats, 0.0) - cross * cross, axis=1, keepdims=True)
     spread = jnp.maximum(squares, 0.0) / 1023.0
     scale = 1.0 / jnp.sqrt(spread + 1e-06)
     for half in range(2):
@@ -274,6 +299,7 @@
     weight_copy.wait_send()
     for b, k in pieces:
         totals_copy(b, k).wait_send()
+    for b, k in ((0, 1), (3, 0), (3, 1)):
         dosage_copy(b, k).wait_send()
     for b in (1, 2, 3):
         gram_copy(b).wait_send()
@@ -291,13 +317,17 @@
 
 def on_device(dosages, weights, variant_pass, ancestry):
     dma = pltpu.SemaphoreType.DMA
-    vmem = pl.BlockSpec(memory_space=pltpu.VMEM)
+    stay = pl.BlockSpec(memory_space=pltpu.HBM)
     return pl.pallas_call(
         kernel,
         out_shape=jax.ShapeDtypeStruct((20, 256), F32),
-        in_specs=[vmem] * 4,
-        out_specs=vmem,
+        in_specs=[stay] * 4,
+        out_specs=pl.BlockSpec(memory_space=pltpu.VMEM),
         scratch_shapes=[
+            pltpu.VMEM((256, 1024), jnp.int32),
+            pltpu.VMEM((256, 2560), BF16),
+            pltpu.VMEM((8, 128), jnp.int32),
+            pltpu.VMEM((20, 256), F32),
             pltpu.VMEM((2, 2560, 256), BF16),
             pltpu.VMEM((4, 2, 128, 256), BF16),
             pltpu.VMEM((4, 2, 128, 256), BF16),
@@ -309,12 +339,13 @@
             pltpu.VMEM((4, 16, 160, 128), BF16),
             pltpu.VMEM((4, 8, 24, 128), F32),
             pltpu.VMEM((2, 16, 24, 128), F32),
-            pltpu.VMEM((256, 128), F32),
-            pltpu.VMEM((24, 128), F32),
-            pltpu.VMEM((4, 24, 128), F32),
             pltpu.VMEM((128, 256), F32),
-            pltpu.VMEM((24, 128), F32),
-            pltpu.VMEM((4, 24, 128), F32),
+            pltpu.VMEM((8, 128), F32),
+            pltpu.VMEM((4, 8, 128), F32),
+            pltpu.VMEM((128, 256), F32),
+            pltpu.VMEM((8, 128), F32),
+            pltpu.VMEM((4, 8, 128), F32),
+            dma((4,)),
             dma((2,)),
             dma((4, 2)), dma((4, 2)), dma((4, 2)), dma((4, 2)),
             dma((4,)), dma((4,)),
@@ -323,10 +354,10 @@
             dma((4,)), dma((4,)),
         ],
         compiler_params=pltpu.CompilerParams(
-            collective_id=0, has_side_effects=True, vmem_limit_bytes=40 << 20
+            collective_id=0, has_side_effects=True, vmem_limit_bytes=64 << 20
         ),
         name="polygenic",
-    )(dosages, weights, variant_pass.reshape(8, 128), ancestry)
+    )(dosages, weights, variant_pass.reshape(8, 128), ancestry.T)
 
 
 def solution(mesh):

time: 100 us -> 85.4 us (0.85)
  the two profiles are of different devices: /device:TPU:38 before, /device:TPU:1 now
where the time goes in v2:
time: 85.4 us; the launch traced here: 85 us
  Pallas kernels  83.6 us (98%)
  local copies, waits for them, and re-layouts  1.35 us (2%)
    pallas_call x1, Pallas kernels, on_device(): pl.pallas_call(kernel, out_shape=jax.ShapeDtypeStruct((20, 256), F32), in...  83.6 us

profile of v2, /device:TPU:1, one launch (start us, length us, event | category | flops | bytes accessed | tf_op | source)
XLA Modules:
  0.0 85.0 jit_solution(5073462587348970377)
XLA Ops:
  0.0 83.6 %polygenic.1 = f32[20,256]{1,0:T(8,128)} custom-call(s32[256,1024]{1,0:T(8,128)} %dos_hbm.1, bf16[256,2560]{1,0:T(8,128)(2,1)} %w_hbm.1, s32[8,128]{1,0:T(8,128)} %bitcast.3, f32[20,256]{1,0:T(8,128)} %bitcast.2), custom_call_target="tpu_custom_call" | custom-call | tf_op jit(solution)/shard_map/polygenic/pallas_call | solution.py:321
  83.6 1.3 %copy.6 = f32[20,256]{1,0:T(8,128)} copy(f32[20,256]{1,0:T(8,128)} %polygenic.1) | data formatting | bytes 40960

commit v3 on v2

--- a/solution.py
+++ b/solution.py
@@ -36,8 +36,8 @@
 def kernel(
     dos_hbm, w_hbm, pass_hbm, anc_hbm, out_ref,
     dos_ref, w_ref, pass_ref, anc_ref,
-    wt, ds, dr, ts, tr, vec, geno, s, r, zs, zr, design, gl, gr, qt, st, sr,
-    in_sem, w_sem, d_send, d_recv, t_send, t_recv, g_send, g_recv, xy_send, xy_recv, z_send, z_recv,
+    wt, ds, dr, ts, tr, vec, geno, s, r, zs, zr, zsn, zrn, design, gl, gr, qt, st, sr,
+    in_sem, w_sem, d_send, d_recv, t_send, t_recv, g_send, g_recv, xy_send, xy_recv, z_send, z_recv, zn_recv,
     st_send, st_recv,
 ):
     v, zh = lax.axis_index("var"), lax.axis_index("samp")
@@ -135,6 +135,9 @@
             at(plane, to_zh * 4 + zl, to_core),
         )
 
+    def dosage_to(b, to_core):
+        return dosage_copy(b, lax.rem(core + to_core, 2))
+
     def small_copy(b, src, dst, send, recv):
         to_zh = lax.rem(zh + 4 - OFFSETS[b], 4)
         return remote(src, dst.at[b], send.at[b], recv.at[b], at(plane, to_zh * 4 + zl, core))
@@ -151,9 +154,9 @@
         totals_copy(b, k).start()
     dosage_copy(0, 1).start()
     weight_copy.start()
-    for k in range(2):
+    for upper in range(2):
         for b in (1, 2):
-            dosage_copy(b, k).start()
+            dosage_to(b, upper).start()
     for b in (1, 2, 3):
         gram_copy(b).start()
 
@@ -207,8 +210,12 @@
 
     def z_copy(b, group):
         to_zh = lax.rem(zh + OFFSETS[b], 4)
+        if b == 3:
+            src, dst, arrived = zsn.at[group], zrn.at[core, zl], zn_recv.at[core, zl]
+        else:
+            src, dst, arrived = zs.at[b, group], zr.at[core, z], z_recv.at[core, z]
         return remote(
-            zs.at[b, group], zr.at[core, z], z_send.at[b, group], z_recv.at[core, z],
+            src, dst, z_send.at[b, group], arrived,
             at(plane, to_zh * 4 + group // 2, lax.rem(group, 2)),
         )
 
@@ -223,9 +230,13 @@
         for step in range(1, 16):
             total += r[b, step].astype(F32)
         for group in range(8):
-            zs[b, group] = jnp.concatenate(
+            part = jnp.concatenate(
                 [total[group * 20 : group * 20 + 20], jnp.zeros((4, 128), F32)], axis=0
             )
+            if b == 3:
+                zsn[group] = part.astype(BF16)
+            else:
+                zs[b, group] = part
         if b == 0:
             zr[core, z] = zs[0, mine]
 
@@ -236,10 +247,11 @@
 
     multiply(0)
     for b in (1, 2):
-        for k in range(2):
-            dosage_copy(b, k).wait_send()
-    for k in range(2):
-        dosage_copy(3, k).start()
+        dosage_to(b, 0).wait_send()
+    dosage_to(3, 0).start()
+    for b in (1, 2):
+        dosage_to(b, 1).wait_send()
+    dosage_to(3, 1).start()
     for b in (1, 2, 3):
         gram_copy(b).wait_recv()
     inverse = inverse_factor(unpack(gl[...] + gr[1] + gr[2] + gr[3]))
@@ -257,20 +269,34 @@
     reduce_plane(3)
     send_along(3)
 
-    @pl.loop(1, 32)
-    def _(step):
-        other = lax.rem(z * 2 + core + step, 32)
-        z_from, core_from = other // 2, lax.rem(other, 2)
+    for part in range(3):
+        from_zh = lax.rem(zh + (0, 1, 3)[part], 4)
+
+        @pl.loop(0 if part else 1, 8)
+        def _(step):
+            other = lax.rem(mine + step, 8)
+            slot = (lax.rem(other, 2), from_zh * 4 + other // 2)
+            remote(
+                zs.at[0, 0], zr.at[slot], z_send.at[0, 0], z_recv.at[slot], at(plane, z, 1 - core)
+            ).wait_recv()
+
+    @pl.loop(0, 8)
+    def _(other):
+        slot = (lax.rem(other, 2), other // 2)
         remote(
-            zs.at[0, 0], zr.at[core_from, z_from], z_send.at[0, 0],
-            z_recv.at[core_from, z_from], at(plane, z, 1 - core),
+            zsn.at[0], zrn.at[slot], z_send.at[0, 0], zn_recv.at[slot], at(plane, z, 1 - core)
         ).wait_recv()
 
     raw = []
     for half in range(2):
-        total = zr[half, 0]
-        for source in range(1, 16):
-            total += zr[half, source]
+        total = zr[half, zh * 4]
+        for source in range(1, 4):
+            total += zr[half, zh * 4 + source]
+        for shift in (1, 3):
+            for source in range(4):
+                total += zr[half, lax.rem(zh + shift, 4) * 4 + source]
+        for source in range(4):
+            total += zrn[half, source].astype(F32)
         raw.append(total)
     cross = jnp.zeros((24, 128), F32)
     squares = jnp.zeros((24, 1), F32)
@@ -337,8 +363,10 @@
             pltpu.VMEM((2, 128, 256), BF16),
             pltpu.VMEM((4, 2560, 128), BF16),
             pltpu.VMEM((4, 16, 160, 128), BF16),
-            pltpu.VMEM((4, 8, 24, 128), F32),
+            pltpu.VMEM((3, 8, 24, 128), F32),
             pltpu.VMEM((2, 16, 24, 128), F32),
+            pltpu.VMEM((8, 24, 128), BF16),
+            pltpu.VMEM((2, 4, 24, 128), BF16),
             pltpu.VMEM((128, 256), F32),
             pltpu.VMEM((8, 128), F32),
             pltpu.VMEM((4, 8, 128), F32),
@@ -350,14 +378,17 @@
             dma((4, 2)), dma((4, 2)), dma((4, 2)), dma((4, 2)),
             dma((4,)), dma((4,)),
             dma((4, 16)), dma((4, 16)),
-            dma((4, 8)), dma((2, 16)),
+            dma((4, 8)), dma((2, 16)), dma((2, 4)),
             dma((4,)), dma((4,)),
         ],
         compiler_params=pltpu.CompilerParams(
-            collective_id=0, has_side_effects=True, vmem_limit_bytes=64 << 20
+            collective_id=0, has_side_effects=True, vmem_limit_bytes=40 << 20
         ),
         name="polygenic",
-    )(dosages, weights, variant_pass.reshape(8, 128), ancestry.T)
+    )(*(
+        pltpu.with_memory_space_constraint(array, pltpu.HBM)
+        for array in (dosages, weights, variant_pass.reshape(8, 128), ancestry.T)
+    ))
 
 
 def solution(mesh):

time: 85.4 us -> 82.1 us (0.961)
  Pallas kernels: 83.6 us -> 81.3 us
    pallas_call x1, Pallas kernels: 83.6 us -> 81.3 us  [on_device(): pl.pallas_call(kernel, out_shape=jax.ShapeDtypeStruct((20, 256), F32), in...]
where the time goes in v3:
time: 82.1 us; the launch traced here: 81.9 us
  Pallas kernels  81.3 us (99%)
    pallas_call x1, Pallas kernels, on_device(): pl.pallas_call(kernel, out_shape=jax.ShapeDtypeStruct((20, 256), F32), in...  81.3 us

profile of v3, /device:TPU:1, one launch (start us, length us, event | category | flops | bytes accessed | tf_op | source)
XLA Modules:
  0.0 81.9 jit_solution(3543412213044053762)
XLA Ops:
  0.0 81.3 %polygenic.1 = f32[20,256]{1,0:T(8,128)S(1)} custom-call(s32[256,1024]{1,0:T(8,128)} %dos_hbm.1, bf16[256,2560]{1,0:T(8,128)(2,1)} %w_hbm.1, s32[8,128]{1,0:T(8,128)} %bitcast.3, f32[20,256]{1,0:T(8,128)} %bitcast.2), custom_call_target="tpu_custom_call" | custom-call | tf_op jit(solution)/shard_map/polygenic/pallas_call | solution.py:347
  81.3 0.6 copy.6

commit v4 on v3

--- a/solution.py
+++ b/solution.py
@@ -35,9 +35,9 @@
 
 def kernel(
     dos_hbm, w_hbm, pass_hbm, anc_hbm, out_ref,
-    dos_ref, w_ref, pass_ref, anc_ref,
+    dos_ref, w_ref, pass_ref, pass_other, anc_ref,
     wt, ds, dr, ts, tr, vec, geno, s, r, zs, zr, zsn, zrn, design, gl, gr, qt, st, sr,
-    in_sem, w_sem, d_send, d_recv, t_send, t_recv, g_send, g_recv, xy_send, xy_recv, z_send, z_recv, zn_recv,
+    in_sem, p_sem, w_sem, d_send, d_recv, t_send, t_recv, g_send, g_recv, xy_send, xy_recv, z_send, z_recv, zn_recv,
     st_send, st_recv,
 ):
     v, zh = lax.axis_index("var"), lax.axis_index("samp")
@@ -99,10 +99,6 @@
         for half in range(2):
             ts[part, half : half + 1, :] = tile[half][0]
             ts[part, 2 + half : 3 + half, :] = tile[half][1]
-            ts[part, 4 + half : 5 + half, :] = pass_ref[
-                2 * part + half : 2 * part + half + 1, :
-            ].astype(F32)
-            ts[part, 6 + half : 7 + half, :] = jnp.zeros((1, 128), F32)
     loads[2].wait()
     design[...] = jnp.zeros_like(design)
     for row in (0, 64):
@@ -149,26 +145,27 @@
         return small_copy(b, st, sr, st_send, st_recv)
 
     pieces = [(b, k) for b in (3, 1, 2, 0) for k in range(2) if b or k]
+    pass_copy = remote(pass_ref, pass_other, p_sem.at[0], p_sem.at[1], at(plane, z, 1 - core))
     weight_copy = remote(wt.at[0], wt.at[1], w_sem.at[0], w_sem.at[1], at(plane, z, 1 - core))
     for b, k in pieces:
         totals_copy(b, k).start()
+    pass_copy.start()
     dosage_copy(0, 1).start()
     weight_copy.start()
     for upper in range(2):
         for b in (1, 2):
             dosage_to(b, upper).start()
-    for b in (1, 2, 3):
-        gram_copy(b).start()
 
     for b, k in pieces:
         totals_copy(b, k).wait_recv()
+    pass_copy.wait_recv()
     for k in range(2):
         total = tr[0, k] + tr[1, k] + tr[2, k] + tr[3, k]
         for half in range(2):
             impute = (total[half : half + 1] + 1.0) / (total[2 + half : 3 + half] + 1.0)
             impute = impute.astype(BF16).astype(F32)
             centre = jnp.floor(impute * 4.0 + 0.5) * 0.25
-            passed = tr[0, k, 4 + half : 5 + half, :]
+            passed = (pass_other if k else pass_ref)[pl.ds(2 * zh + half, 1), :].astype(F32)
             vec[k, half, 0:1, :] = centre
             vec[k, half, 1:2, :] = (impute - centre) * passed
             vec[k, half, 2:3, :] = passed
@@ -180,7 +177,7 @@
             xy_send.at[b, dy * 4 + dx], xy_recv.at[b, dy * 4 + dx], at(to, z, core),
         )
 
-    def multiply(b):
+    def multiply(b, arrived=None):
         for k in range(2):
             if b or k:
                 dosage_copy(b, k).wait_recv()
@@ -191,6 +188,8 @@
                 geno[k, :, pl.ds(half * 128, 128)] = jnp.where(
                     dose < 2.5, (dose - centre) * passed, missing
                 ).astype(BF16)
+        if arrived is not None:
+            arrived()
         if b == 0:
             weight_copy.wait_recv()
 
@@ -246,26 +245,24 @@
             z_copy(b, lax.rem(mine + step, 8)).start()
 
     multiply(0)
-    for b in (1, 2):
-        dosage_to(b, 0).wait_send()
     dosage_to(3, 0).start()
-    for b in (1, 2):
-        dosage_to(b, 1).wait_send()
     dosage_to(3, 1).start()
+    for b in (1, 2, 3):
+        gram_copy(b).start()
+    multiply(1)
+    multiply(2)
+    reduce_plane(0)
+    send_along(0)
+    reduce_plane(1)
+    multiply(3)
+    send_along(1)
+    reduce_plane(2)
+    send_along(2)
     for b in (1, 2, 3):
         gram_copy(b).wait_recv()
     inverse = inverse_factor(unpack(gl[...] + gr[1] + gr[2] + gr[3]))
     qt[...] = jnp.zeros_like(qt)
     qt[0:24, :] = jnp.dot(inverse, design[...], precision=HI, preferred_element_type=F32)
-    multiply(1)
-    multiply(2)
-    reduce_plane(0)
-    reduce_plane(1)
-    multiply(3)
-    send_along(0)
-    send_along(1)
-    reduce_plane(2)
-    send_along(2)
     reduce_plane(3)
     send_along(3)
 
@@ -322,10 +319,11 @@
         )
         out_ref[:, pl.ds(half * 128, 128)] = ((raw[half] - fitted) * scale)[0:20]
 
+    pass_copy.wait_send()
     weight_copy.wait_send()
     for b, k in pieces:
         totals_copy(b, k).wait_send()
-    for b, k in ((0, 1), (3, 0), (3, 1)):
+    for b, k in pieces:
         dosage_copy(b, k).wait_send()
     for b in (1, 2, 3):
         gram_copy(b).wait_send()
@@ -353,12 +351,13 @@
             pltpu.VMEM((256, 1024), jnp.int32),
             pltpu.VMEM((256, 2560), BF16),
             pltpu.VMEM((8, 128), jnp.int32),
+            pltpu.VMEM((8, 128), jnp.int32),
             pltpu.VMEM((20, 256), F32),
             pltpu.VMEM((2, 2560, 256), BF16),
             pltpu.VMEM((4, 2, 128, 256), BF16),
             pltpu.VMEM((4, 2, 128, 256), BF16),
-            pltpu.VMEM((4, 8, 128), F32),
-            pltpu.VMEM((4, 2, 8, 128), F32),
+            pltpu.VMEM((4, 4, 128), F32),
+            pltpu.VMEM((4, 2, 4, 128), F32),
             pltpu.VMEM((2, 2, 8, 128), F32),
             pltpu.VMEM((2, 128, 256), BF16),
             pltpu.VMEM((4, 2560, 128), BF16),
@@ -375,6 +374,7 @@
             pltpu.VMEM((4, 8, 128), F32),
             dma((4,)),
             dma((2,)),
+            dma((2,)),
             dma((4, 2)), dma((4, 2)), dma((4, 2)), dma((4, 2)),
             dma((4,)), dma((4,)),
             dma((4, 16)), dma((4, 16)),

time: 82.1 us -> 78.3 us (0.954)
  the two profiles are of different devices: /device:TPU:1 before, /device:TPU:32 now
where the time goes in v4:
time: 78.3 us; the launch traced here: 78.1 us
  Pallas kernels  77.5 us (99%)
    pallas_call x1, Pallas kernels, on_device(): pl.pallas_call(kernel, out_shape=jax.ShapeDtypeStruct((20, 256), F32), in...  77.5 us

profile of v4, /device:TPU:32, one launch (start us, length us, event | category | flops | bytes accessed | tf_op | source)
XLA Modules:
  0.0 78.1 jit_solution(5344451630681053563)
XLA Ops:
  0.0 77.5 %polygenic.1 = f32[20,256]{1,0:T(8,128)S(1)} custom-call(s32[256,1024]{1,0:T(8,128)} %dos_hbm.1, bf16[256,2560]{1,0:T(8,128)(2,1)} %w_hbm.1, s32[8,128]{1,0:T(8,128)} %bitcast.3, f32[20,256]{1,0:T(8,128)} %bitcast.2), custom_call_target="tpu_custom_call" | custom-call | tf_op jit(solution)/shard_map/polygenic/pallas_call | solution.py:345
  77.5 0.6 copy.6

commit v5 on v4

--- a/solution.py
+++ b/solution.py
@@ -152,9 +152,8 @@
     pass_copy.start()
     dosage_copy(0, 1).start()
     weight_copy.start()
-    for upper in range(2):
-        for b in (1, 2):
-            dosage_to(b, upper).start()
+    for b in (1, 2, 3):
+        dosage_to(b, 0).start()
 
     for b, k in pieces:
         totals_copy(b, k).wait_recv()
@@ -221,12 +220,9 @@
     mine = zl * 2 + core
 
     def reduce_plane(b):
-        @pl.loop(1, 16)
-        def _(step):
-            xy_copy(b, step // 4, lax.rem(step, 4)).wait_recv()
-
         total = s[b, pl.ds(pl.multiple_of(plane * 160, 160), 160), :].astype(F32)
-        for step in range(1, 16):
+        for step in (1, 3, 4, 12, 2, 8, 5, 7, 13, 15, 6, 9, 11, 14, 10):
+            xy_copy(b, step // 4, step % 4).wait_recv()
             total += r[b, step].astype(F32)
         for group in range(8):
             part = jnp.concatenate(
@@ -244,13 +240,14 @@
         def _(step):
             z_copy(b, lax.rem(mine + step, 8)).start()
 
+    for b in (1, 2):
+        dosage_to(b, 1).start()
     multiply(0)
-    dosage_to(3, 0).start()
     dosage_to(3, 1).start()
-    for b in (1, 2, 3):
-        gram_copy(b).start()
     multiply(1)
     multiply(2)
+    for b in (1, 2, 3):
+        gram_copy(b).start()
     reduce_plane(0)
     send_along(0)
     reduce_plane(1)
@@ -276,13 +273,6 @@
             remote(
                 zs.at[0, 0], zr.at[slot], z_send.at[0, 0], z_recv.at[slot], at(plane, z, 1 - core)
             ).wait_recv()
-
-    @pl.loop(0, 8)
-    def _(other):
-        slot = (lax.rem(other, 2), other // 2)
-        remote(
-            zsn.at[0], zrn.at[slot], z_send.at[0, 0], zn_recv.at[slot], at(plane, z, 1 - core)
-        ).wait_recv()
 
     raw = []
     for half in range(2):
@@ -292,17 +282,19 @@
         for shift in (1, 3):
             for source in range(4):
                 total += zr[half, lax.rem(zh + shift, 4) * 4 + source]
-        for source in range(4):
-            total += zrn[half, source].astype(F32)
         raw.append(total)
-    cross = jnp.zeros((24, 128), F32)
-    squares = jnp.zeros((24, 1), F32)
-    for half in range(2):
-        cross += lax.dot_general(
-            raw[half], qt[:, pl.ds(half * 128, 128)], LANES_TO_LANES, precision=HI,
-            preferred_element_type=F32,
-        )
-        squares += jnp.sum(raw[half] * raw[half], axis=1, keepdims=True)
+    raw = jnp.concatenate(raw, axis=1)
+    for source in range(4):
+        for half in range(2):
+            remote(
+                zsn.at[0], zrn.at[half, source], z_send.at[0, 0], zn_recv.at[half, source],
+                at(plane, z, 1 - core),
+            ).wait_recv()
+        raw += jnp.concatenate([zrn[0, source], zrn[1, source]], axis=1).astype(F32)
+    cross = lax.dot_general(
+        raw, qt[...], LANES_TO_LANES, precision=HI, preferred_element_type=F32
+    )
+    squares = jnp.sum(raw * raw, axis=1, keepdims=True)
     st[...] = pack(jnp.where(lane == 24, squares, cross))
     for b in (3, 1, 2):
         stat_copy(b).start()
@@ -313,11 +305,8 @@
     squares = jnp.sum(jnp.where(lane == 24, stats, 0.0) - cross * cross, axis=1, keepdims=True)
     spread = jnp.maximum(squares, 0.0) / 1023.0
     scale = 1.0 / jnp.sqrt(spread + 1e-06)
-    for half in range(2):
-        fitted = jnp.dot(
-            cross, qt[:, pl.ds(half * 128, 128)], precision=HI, preferred_element_type=F32
-        )
-        out_ref[:, pl.ds(half * 128, 128)] = ((raw[half] - fitted) * scale)[0:20]
+    fitted = jnp.dot(cross, qt[...], precision=HI, preferred_element_type=F32)
+    out_ref[...] = ((raw - fitted) * scale)[0:20]
 
     pass_copy.wait_send()
     weight_copy.wait_send()

time: 78.3 us -> 77.2 us (0.986)
  the two profiles are of different devices: /device:TPU:32 before, /device:TPU:1 now
where the time goes in v5:
time: 77.2 us; the launch traced here: 77.1 us
  Pallas kernels  76.5 us (99%)
    pallas_call x1, Pallas kernels, on_device(): pl.pallas_call(kernel, out_shape=jax.ShapeDtypeStruct((20, 256), F32), in...  76.5 us

profile of v5, /device:TPU:1, one launch (start us, length us, event | category | flops | bytes accessed | tf_op | source)
XLA Modules:
  0.0 77.1 jit_solution(18427486662534606580)
XLA Ops:
  0.0 76.5 %polygenic.1 = f32[20,256]{1,0:T(8,128)S(1)} custom-call(s32[256,1024]{1,0:T(8,128)} %dos_hbm.1, bf16[256,2560]{1,0:T(8,128)(2,1)} %w_hbm.1, s32[8,128]{1,0:T(8,128)} %bitcast.3, f32[20,256]{1,0:T(8,128)} %bitcast.2), custom_call_target="tpu_custom_call" | custom-call | tf_op jit(solution)/shard_map/polygenic/pallas_call | solution.py:334
  76.5 0.6 copy.6

commit v6 on v5

--- a/solution.py
+++ b/solution.py
@@ -248,10 +248,10 @@
     multiply(2)
     for b in (1, 2, 3):
         gram_copy(b).start()
+    multiply(3)
     reduce_plane(0)
     send_along(0)
     reduce_plane(1)
-    multiply(3)
     send_along(1)
     reduce_plane(2)
     send_along(2)

time: 77.2 us -> 77 us (level)
  no operation moved by 1% of the time
where the time goes in v6:
time: 77 us; the launch traced here: 76.5 us
  Pallas kernels  75.9 us (99%)
    pallas_call x1, Pallas kernels, on_device(): pl.pallas_call(kernel, out_shape=jax.ShapeDtypeStruct((20, 256), F32), in...  75.9 us

profile of v6, /device:TPU:1, one launch (start us, length us, event | category | flops | bytes accessed | tf_op | source)
XLA Modules:
  0.0 76.5 jit_solution(2085722299144661431)
XLA Ops:
  0.0 75.9 %polygenic.1 = f32[20,256]{1,0:T(8,128)S(1)} custom-call(s32[256,1024]{1,0:T(8,128)} %dos_hbm.1, bf16[256,2560]{1,0:T(8,128)(2,1)} %w_hbm.1, s32[8,128]{1,0:T(8,128)} %bitcast.3, f32[20,256]{1,0:T(8,128)} %bitcast.2), custom_call_target="tpu_custom_call" | custom-call | tf_op jit(solution)/shard_map/polygenic/pallas_call | solution.py:334
  75.9 0.6 copy.6
